TPU v7x, 128 devices: a whole 4x4x4 slice. The times are simulated.
128 devices in a mesh: chan: 32 (over z_lo, y, x), seg: 4 (over z_hi, core).
Axes of the slice: x: 4, y: 4, z: 4 (z_hi: 2, z_lo: 2; z = z_hi * 2 + z_lo), core: 2. Of those that a mesh axis runs over, the one named last changes fastest.
Arguments:
- traces: bfloat16 [4096, 8, 8192], P('chan', 'seg'), may hold values from -20 to 20
- pair_offsets: int32 [32, 16], replicated, may hold values from 1 to 31, as said below
- pair_counts: int32 [32], replicated, may hold values from 1 to 16, 64 in all
- pair_owner: int32 [64], replicated, may hold values from 0 to 63, each once
Outputs:
- correlations: float32 [128, 64, 128, 256], P('seg', 'chan')
Inputs may be any that keep to these rules, and one draw needn't show every extreme that they name: `pair_offsets`: row a lists 16 distinct offsets; only its first pair_counts[a] entries name pairs. `pair_counts`: the counts sum to 64. `pair_owner`: every slot number appears once.
All inputs are finite; a program needn't handle non-finite values.
Results may differ from a plain program's by a relative error of at most 0.017.
Values may be sent and summed in bfloat16 or wider, within the bound.
No kernel may reach another device: no remote copies, remote signals or barrier semaphores. Data moves between devices by JAX's collectives and lax.ppermute only.
A program may use at most 128 MiB of HBM per device.

v0:
```python
import math
import jax
import jax.numpy as jnp
from jax import lax
from jax.sharding import PartitionSpec as P

SAMPLES = 8192
BAND_START = 32
FREQS = 512
HALF = 8
LAGS = 256
TILE_DEV = 2


def smoother(bin_count):
    bins_axis = lax.iota(jnp.int32, bin_count)
    nearby = (jnp.abs(bins_axis[:, None] - bins_axis[None, :]) <= HALF).astype(jnp.float32)
    return nearby / jnp.sum(nearby, axis=0, keepdims=True)


def lag_table(first_bin, bin_count):
    bins_axis = BAND_START + first_bin + lax.iota(jnp.int32, bin_count)
    shifts = jnp.mod(lax.iota(jnp.int32, LAGS) - LAGS // 2, SAMPLES)
    phase_index = jnp.mod(bins_axis[:, None] * shifts[None, :], SAMPLES)
    angles = phase_index.astype(jnp.float32) * (2.0 * math.pi / SAMPLES)
    return jnp.concatenate([jnp.cos(angles), -jnp.sin(angles)], axis=0).astype(jnp.bfloat16)


def pair_blocks(pair_offsets, pair_counts, pair_owner, block_count, slot_count):
    slot_index = lax.iota(jnp.int32, slot_count)
    starts = jnp.cumsum(pair_counts) - pair_counts
    first_block = jnp.sum((starts[None, :] <= slot_index[:, None]).astype(jnp.int32), axis=1) - 1
    member = lax.iota(jnp.int32, block_count)[None, :] == first_block[:, None]
    start_of = jnp.sum(jnp.where(member, starts[None, :], 0), axis=1)
    position = slot_index - start_of
    listed = jnp.sum(jnp.where(member[:, :, None], pair_offsets[None, :, :], 0), axis=1)
    chosen = lax.iota(jnp.int32, pair_offsets.shape[1])[None, :] == position[:, None]
    offset = jnp.sum(jnp.where(chosen, listed, 0), axis=1)
    second_block = jnp.mod(first_block + offset, block_count)
    held = pair_owner[None, :] == slot_index[:, None]
    slot_first = jnp.sum(jnp.where(held, first_block[None, :], 0), axis=1)
    slot_second = jnp.sum(jnp.where(held, second_block[None, :], 0), axis=1)
    return (slot_first, slot_second)


def cross_terms(first_spec, second_spec):
    turned = jnp.stack([first_spec[:, :, :, 1], -first_spec[:, :, :, 0]], axis=3)
    real_part = jnp.einsum(
        "tispf,tjspf->itjf", first_spec, second_spec, preferred_element_type=jnp.float32
    )
    imag_part = jnp.einsum(
        "tispf,tjspf->itjf", turned, second_spec, preferred_element_type=jnp.float32
    )
    return jnp.stack([real_part, imag_part], axis=3).astype(jnp.bfloat16)


def invert(spectra, table, norm_factor):
    flat = spectra.reshape(-1, spectra.shape[3] * spectra.shape[4])
    lagged = jnp.dot(flat, table, preferred_element_type=jnp.float32) * norm_factor
    return lagged.reshape(spectra.shape[:3] + (table.shape[1],))


def on_device(traces, pair_offsets, pair_counts, pair_owner):
    block_size, local_segs, sample_count = traces.shape
    parts_count = lax.axis_size("seg")
    block_count = lax.axis_size("chan")
    quarter_bins = FREQS // parts_count
    all_segs = local_segs * parts_count
    norm_factor = 1.0 / math.sqrt(FREQS * all_segs)
    signal = traces.reshape(block_size * local_segs, sample_count)
    width_bins = min(128, FREQS)
    pieces_count = FREQS // width_bins
    times_axis = lax.iota(jnp.int32, sample_count)

    def transform(piece_index):
        bins_axis = BAND_START + piece_index * width_bins + lax.iota(jnp.int32, width_bins)
        phase_index = jnp.mod(times_axis[:, None] * bins_axis[None, :], sample_count)
        angles = phase_index.astype(jnp.float32) * (2.0 * math.pi / sample_count)
        table_part = jnp.concatenate([jnp.cos(angles), -jnp.sin(angles)], axis=1)
        table_high = table_part.astype(jnp.bfloat16)
        table_low = (table_part - table_high.astype(jnp.float32)).astype(jnp.bfloat16)
        upper = jnp.dot(signal, table_high, preferred_element_type=jnp.float32)
        return upper + jnp.dot(signal, table_low, preferred_element_type=jnp.float32)

    spectrum = lax.map(transform, lax.iota(jnp.int32, pieces_count))
    spectrum = (
        spectrum.reshape(pieces_count, -1, 2, width_bins)
        .transpose(1, 2, 0, 3)
        .reshape(-1, 2, FREQS)
    )
    real_part = spectrum[:, 0]
    imag_part = spectrum[:, 1]
    amplitude = jnp.sqrt(real_part * real_part + imag_part * imag_part)
    smoothed = jnp.dot(
        amplitude,
        smoother(FREQS),
        precision=lax.Precision.HIGHEST,
        preferred_element_type=jnp.float32,
    )
    divisor = jnp.maximum(smoothed, 1.0)
    whitened = jnp.stack([real_part / divisor, imag_part / divisor], axis=1).astype(jnp.bfloat16)
    whitened = whitened.reshape(block_size, local_segs, 2, parts_count, quarter_bins)
    quarter = lax.all_to_all(whitened, "seg", split_axis=3, concat_axis=1, tiled=True)
    quarter = quarter.reshape(block_size, all_segs, 2, quarter_bins)
    slot_first, slot_second = pair_blocks(
        pair_offsets, pair_counts, pair_owner, block_count, TILE_DEV * block_count
    )
    my_start = lax.axis_index("chan") * TILE_DEV
    needed = jnp.concatenate(
        [
            lax.dynamic_slice_in_dim(slot_first, my_start, TILE_DEV),
            lax.dynamic_slice_in_dim(slot_second, my_start, TILE_DEV),
        ]
    )
    empty_blocks = jnp.zeros((2 * TILE_DEV, block_size, all_segs, 2, quarter_bins), jnp.bfloat16)
    incoming = lax.all_gather(quarter, "chan", axis=0, tiled=True)
    block_total = incoming.shape[0] // block_size
    incoming_blocks = incoming.reshape(block_total, block_size, all_segs, 2, quarter_bins)
    inside = (needed >= 0) & (needed < block_total)
    picked = jnp.take(incoming_blocks, jnp.clip(needed, 0, block_total - 1), axis=0)
    held_blocks = jnp.where(inside[:, None, None, None, None], picked, empty_blocks)
    first_spec = held_blocks[:TILE_DEV]
    second_spec = held_blocks[TILE_DEV:]
    full_table = lag_table(0, FREQS)
    spectra = cross_terms(first_spec, second_spec)
    return invert(
        lax.all_to_all(spectra, "seg", split_axis=0, concat_axis=4, tiled=True),
        full_table,
        norm_factor,
    )


def solution(mesh):
    placed = (P("chan", "seg", None), P(), P(), P())
    return jax.shard_map(
        on_device,
        mesh=mesh,
        in_specs=placed,
        out_specs=P("seg", "chan", None, None),
        check_vma=False,
    )
```

profile of v0, /device:TPU:1, one launch (start us, length us, event | category | flops | bytes accessed | tf_op | source)
XLA Modules:
  0.0 643.9 jit_solution(6079321119400441198)
XLA Ops:
  6.5 0.1 convert_reduce_fusion
  6.6 7.2 %reshape.215 = bf16[256,8192]{1,0:T(8,128)(2,1)} reshape(bf16[128,2,8192]{2,1,0:T(2,128)(2,1)} %param.6) | data formatting | bytes 8388608 | tf_op jit(solution)/shard_map/reshape | solution.py:70
  13.8 82.4 %while.13 = (s32[]{:T(128)}, f32[4,256,256]{1,2,0:T(8,128)S(1)}, s32[4]{0:T(128)S(1)}, bf16[256,8192]{1,0:T(8,128)(2,1)}, s32[]{:T(128)}, /*index=5*/s32[1]{0:T(128)}, s32[1]{0:T(128)}) while((s32[]{:T(128)}, f32[4,256,256]{1,2,0:T(8,128)S(1)}, s32[4]{0:T(128)S(1)}, bf16[256,8192]{1,0:T(8,128)(2,1)}, s32[]{:T(128)}, ...), condition=%wide.region_8.9_spmd.clone, body=%wide.region_7.8_spmd.clone.sunk | while | flops 2182152192 | bytes 51119252 | solution.py:85
  13.8 0.7 dynamic_slice.19
  15.2 0.0 copy-start
  15.2 16.5 %fusion.57 = (f32[8192,128]{1,0:T(8,128)S(1)}, f32[8192,128]{1,0:T(8,128)S(1)}) fusion(s32[128]{0:T(128)S(1)} %iota_add_fusion.3), kind=kLoop, calls=%fused_computation.18.clone.1 | loop fusion | flops 15728640 | bytes 8389120 | tf_op jit(solution)/shard_map/while/body/eval_jaxpr/cos | solution.py:79
  31.7 1.3 fusion.58
  33.0 1.3 fusion.59
  34.4 0.7 dynamic_slice.19
  35.7 0.0 copy-start
  35.7 16.5 %fusion.57 = (f32[8192,128]{1,0:T(8,128)S(1)}, f32[8192,128]{1,0:T(8,128)S(1)}) fusion(s32[128]{0:T(128)S(1)} %iota_add_fusion.3), kind=kLoop, calls=%fused_computation.18.clone.1 | loop fusion | flops 15728640 | bytes 8389120 | tf_op jit(solution)/shard_map/while/body/eval_jaxpr/cos | solution.py:79
  52.3 1.3 fusion.58
  53.6 1.3 fusion.59
  54.9 0.7 dynamic_slice.19
  56.3 0.0 copy-start
  56.3 16.5 %fusion.57 = (f32[8192,128]{1,0:T(8,128)S(1)}, f32[8192,128]{1,0:T(8,128)S(1)}) fusion(s32[128]{0:T(128)S(1)} %iota_add_fusion.3), kind=kLoop, calls=%fused_computation.18.clone.1 | loop fusion | flops 15728640 | bytes 8389120 | tf_op jit(solution)/shard_map/while/body/eval_jaxpr/cos | solution.py:79
  72.8 1.3 fusion.58
  74.1 1.3 fusion.59
  75.5 0.7 dynamic_slice.19
  76.8 0.0 copy-start
  76.9 16.5 %fusion.57 = (f32[8192,128]{1,0:T(8,128)S(1)}, f32[8192,128]{1,0:T(8,128)S(1)}) fusion(s32[128]{0:T(128)S(1)} %iota_add_fusion.3), kind=kLoop, calls=%fused_computation.18.clone.1 | loop fusion | flops 15728640 | bytes 8389120 | tf_op jit(solution)/shard_map/while/body/eval_jaxpr/cos | solution.py:79
  93.4 1.3 fusion.58
  94.7 1.3 fusion.59
  96.2 0.4 copy.29
  96.6 0.4 reshape.217
  97.0 1.2 divide_convert_fusion.1
  98.2 0.0 copy-start.2
  98.2 0.0 copy-start.1
  98.3 0.0 copy-start.3
  98.3 0.1 stack.25
  98.4 0.1 stack.26
  98.5 0.1 pad_maximum_fusion.2
  98.6 15.9 %all_to_all.30 = bf16[128,2,2,4,128]{4,0,2,1,3:T(8,128)(2,1)} all-to-all(bf16[128,2,2,4,128]{4,0,2,1,3:T(8,128)(2,1)S(1)} %pad_maximum_fusion.2), channel_id=1, replica_groups=mesh['chan'=32,'seg'=4] {'seg'}, dimensions={3} | all-to-all | bytes 1048576 | tf_op jit(solution)/shard_map/all_to_all | solution.py:103
  114.4 0.0 all-gather.2.cloned.1.call-update
  114.5 0.1 copy.27
  114.6 0.1 reduce-window.9
  114.6 0.1 reduce
  114.7 0.1 copy.28
  114.8 0.1 convert_reduce_fusion.1
  114.9 0.1 select_reduce_fusion.3
  115.0 0.1 select_reduce_fusion
  115.2 0.1 select_reduce_fusion.2
  115.3 0.1 dynamic_slice.13
  115.4 0.1 dynamic_slice.14
  115.5 0.1 dynamic-slice_bitcast_fusion
  115.5 0.1 dynamic-slice_bitcast_fusion.1
  115.6 0.1 fusion.38
  115.7 0.1 compare_and_fusion.1
  115.8 186.4 %all-gather.2.cloned.1.call-done = bf16[4096,8,2,128]{3,0,2,1:T(8,128)(2,1)} async-done(((bf16[128,8,2,128]{3,0,2,1:T(8,128)(2,1)}), bf16[4096,8,2,128]{3,0,2,1:T(8,128)(2,1)}) %all-gather.2.cloned.1.call-update) | async-done | bytes 16777232 | tf_op jit(solution)/shard_map/all_gather | solution.py:116
  302.2 18.6 %copy.32 = bf16[4096,8,2,128]{3,1,2,0:T(8,128)(2,1)} copy(bf16[4096,8,2,128]{3,0,2,1:T(8,128)(2,1)} %all-gather.2.cloned.1.call-done) | data formatting | bytes 33554432 | tf_op jit(solution)/shard_map/all_gather | solution.py:116
  320.7 7.9 %gather_fusion = bf16[4,128,8,2,128]{4,2,3,1,0:T(8,128)(2,1)} fusion(bf16[32,128,8,2,128]{4,2,3,1,0:T(8,128)(2,1)} %bitcast.77, s32[1024]{0:T(1024)S(1)} %pad_clamp_fusion), kind=kCustom, calls=%fused_computation | custom fusion | bytes 4194320 | tf_op jit(solution)/shard_map/jit(_take)/gather | solution.py:120
  328.6 4.2 copy.33
  332.9 0.3 select_select_fusion
  333.2 0.1 fusion.42
  333.3 4.9 fusion.18
  338.2 4.9 fusion.19
  343.1 6.8 %pad_maximum_fusion.1 = bf16[128,2,128,2,128]{0,2,4,1,3:T(8,128)(2,1)} fusion(bf16[128,2,128,1,128]{0,2,4,1,3:T(8,128)(2,1)S(1)} %fusion.19, bf16[128,2,128,1,128]{0,2,4,1,3:T(8,128)(2,1)S(1)} %fusion.18), kind=kLoop, calls=%fused_computation.25 | loop fusion | flops 8388608 | bytes 33554432 | tf_op jit(solution)/shard_map/stack | solution.py:54
  349.9 23.5 %copy.34 = bf16[128,2,128,2,128]{2,4,1,3,0:T(8,128)(2,1)} copy(bf16[128,2,128,2,128]{0,2,4,1,3:T(8,128)(2,1)} %pad_maximum_fusion.1) | data formatting | bytes 33554432 | tf_op jit(solution)/shard_map/stack | solution.py:54
  373.4 12.9 %all-to-all-start.1 = ((bf16[128,2,128,2,128]{2,4,1,3,0:T(8,128)(2,1)}), bf16[128,2,128,2,128]{2,4,1,3,0:T(8,128)(2,1)}, u32[]{:S(2)}, u32[]{:S(2)}) async-start(bf16[128,2,128,2,128]{2,4,1,3,0:T(8,128)(2,1)} %copy.34), calls=%async_computation.1 | async-start | bytes 33554432 | tf_op jit(solution)/shard_map/all_to_all | solution.py:127
  386.3 2.5 cosine_convert_fusion
  388.8 181.2 %all-to-all-done.1 = bf16[128,2,128,2,128]{2,4,1,3,0:T(8,128)(2,1)} async-done(((bf16[128,2,128,2,128]{2,4,1,3,0:T(8,128)(2,1)}), bf16[128,2,128,2,128]{2,4,1,3,0:T(8,128)(2,1)}, u32[]{:S(2)}, u32[]{:S(2)}) %all-to-all-start.1) | async-done | bytes 16777248 | tf_op jit(solution)/shard_map/all_to_all | solution.py:127
  570.0 26.0 %copy.36 = bf16[32,2,128,2,4,128]{5,4,3,2,1,0:T(4,128)(2,1)} copy(bf16[32,2,128,2,4,128]{2,5,1,3,0,4:T(8,128)(2,1)} %bitcast.22) | data formatting | bytes 33554432 | tf_op jit(solution)/shard_map/all_to_all | solution.py:127
  596.0 27.3 %reshape.220 = bf16[8192,1024]{1,0:T(8,128)(2,1)} reshape(bf16[32,2,128,2,4,128]{5,4,3,2,1,0:T(4,128)(2,1)} %copy.36) | data formatting | bytes 33554432 | tf_op jit(solution)/shard_map/reshape | solution.py:58
  623.4 13.7 %convolution_multiply_fusion = f32[8192,256]{1,0:T(8,128)} fusion(bf16[8192,1024]{1,0:T(8,128)(2,1)} %reshape.220, bf16[512,256]{1,0:T(8,128)(2,1)S(1)} %get-tuple-element.99, bf16[512,256]{1,0:T(8,128)(2,1)S(1)} %get-tuple-element.98), kind=kOutput, calls=%fused_computation.28 | convolution fusion | flops 4298113024 | bytes 25690112 | tf_op jit(solution)/shard_map/dot_general | solution.py:59
  (25 shorter events, 0.2 us)
Async XLA Ops:
  6.5 295.6 %all-gather.2.cloned.1.call-start = ((), (), s32[]{:S(2)}) async-start(), calls=%async_computation.2 | async-start | bytes 17301504 | tf_op jit(solution)/shard_map/all_gather | solution.py:116
  15.2 16.5 %copy-start = (bf16[256,8192]{1,0:T(8,128)(2,1)S(1)}, bf16[256,8192]{1,0:T(8,128)(2,1)}, u32[]{:S(2)}) copy-start(bf16[256,8192]{1,0:T(8,128)(2,1)} %get-tuple-element.148) | copy-start | bytes 12582916 | tf_op jit(solution)/shard_map/while
  35.7 16.5 %copy-start = (bf16[256,8192]{1,0:T(8,128)(2,1)S(1)}, bf16[256,8192]{1,0:T(8,128)(2,1)}, u32[]{:S(2)}) copy-start(bf16[256,8192]{1,0:T(8,128)(2,1)} %get-tuple-element.148) | copy-start | bytes 12582916 | tf_op jit(solution)/shard_map/while
  56.3 16.5 %copy-start = (bf16[256,8192]{1,0:T(8,128)(2,1)S(1)}, bf16[256,8192]{1,0:T(8,128)(2,1)}, u32[]{:S(2)}) copy-start(bf16[256,8192]{1,0:T(8,128)(2,1)} %get-tuple-element.148) | copy-start | bytes 12582916 | tf_op jit(solution)/shard_map/while
  76.8 16.5 %copy-start = (bf16[256,8192]{1,0:T(8,128)(2,1)S(1)}, bf16[256,8192]{1,0:T(8,128)(2,1)}, u32[]{:S(2)}) copy-start(bf16[256,8192]{1,0:T(8,128)(2,1)} %get-tuple-element.148) | copy-start | bytes 12582916 | tf_op jit(solution)/shard_map/while
  98.2 16.2 %copy-start.2 = (s32[32]{0:T(128)S(1)}, s32[32]{0:T(128)}, u32[]{:S(2)}) copy-start(s32[32]{0:T(128)} %param.8) | copy-start | bytes 388
  98.2 16.5 %copy-start.1 = (s32[32,16]{0,1:T(8,128)S(1)}, s32[32,16]{0,1:T(8,128)}, u32[]{:S(2)}) copy-start(s32[32,16]{0,1:T(8,128)} %param.7) | copy-start | bytes 6148
  98.3 16.9 %copy-start.3 = (s32[64]{0:T(128)S(1)}, s32[64]{0:T(128)}, u32[]{:S(2)}) copy-start(s32[64]{0:T(128)} %param.9) | copy-start | bytes 772
  373.4 196.6 %all-to-all-start.1 = ((bf16[128,2,128,2,128]{2,4,1,3,0:T(8,128)(2,1)}), bf16[128,2,128,2,128]{2,4,1,3,0:T(8,128)(2,1)}, u32[]{:S(2)}, u32[]{:S(2)}) async-start(bf16[128,2,128,2,128]{2,4,1,3,0:T(8,128)(2,1)} %copy.34), calls=%async_computation.1 | async-start | bytes 33554432 | tf_op jit(solution)/shard_map/all_to_all | solution.py:127
Sparse Core Ops, SparseCore 0:
  114.6 187.5 all-gather.1
where the time goes:
time: 647 us; the launch traced here: 644 us
  waiting for transfers between devices  368 us (57%)
  local copies, waits for them, and re-layouts  119 us (18%)
  other arithmetic  76.8 us (12%)
  matrix products  35.1 us (5%)
  blocking collectives  15.9 us (2%)
  between operations  13.6 us (2%)
  starting transfers between devices  12.9 us (2%)
    all_gather x1, waiting for transfers between devices, on_device(): incoming = lax.all_gather(quarter, 'chan', axis=0, tiled=True)  186 us
    all_to_all x1, waiting for transfers between devices, on_device(): lax.all_to_all(spectra, 'seg', split_axis=0, concat_axis=4, tiled=True)  181 us
    cos x4, other arithmetic, transform(): table_part = jnp.concatenate([jnp.cos(angles), -jnp.sin(angles)], axis=1)  66.1 us
    reshape x1, local copies, waits for them, and re-layouts, invert(): flat = spectra.reshape(-1, spectra.shape[3] * spectra.shape[4])  27.3 us
    all_to_all x1, local copies, waits for them, and re-layouts, on_device(): lax.all_to_all(spectra, 'seg', split_axis=0, concat_axis=4, tiled=True)  26 us
    another operation x1, local copies, waits for them, and re-layouts, cross_terms(): return jnp.stack([real_part, imag_part], axis=3).astype(jnp.bfloat16)  23.5 us
    all_gather x1, local copies, waits for them, and re-layouts, on_device(): incoming = lax.all_gather(quarter, 'chan', axis=0, tiled=True)  18.6 us
    all_to_all x1, blocking collectives, on_device(): lax.all_to_all(whitened, 'seg', split_axis=3, concat_axis=1, tiled=True)  15.9 us
  transfers between devices with their start and end apart: 2, of which 2 were waited for; matrix products, arithmetic and copies ran while one was open for 1% of the time, Pallas kernels for 0%

commit v1 on v0

--- a/solution.py
+++ b/solution.py
@@ -113,7 +113,10 @@
         ]
     )
     empty_blocks = jnp.zeros((2 * TILE_DEV, block_size, all_segs, 2, quarter_bins), jnp.bfloat16)
-    incoming = lax.all_gather(quarter, "chan", axis=0, tiled=True)
+    n_dev = lax.axis_size("chan")
+    pieces = jnp.stack([quarter for _ in range(n_dev)])
+    pieces = lax.all_to_all(pieces, "chan", split_axis=0, concat_axis=0)
+    incoming = jnp.concatenate(pieces, axis=0)
     block_total = incoming.shape[0] // block_size
     incoming_blocks = incoming.reshape(block_total, block_size, all_segs, 2, quarter_bins)
     inside = (needed >= 0) & (needed < block_total)

time: 647 us -> 730 us (1.13)
  the two profiles are of different devices: /device:TPU:1 before, /device:TPU:2 now
where the time goes in v1:
time: 730 us; the launch traced here: 727 us
  waiting for transfers between devices  469 us (64%)
  local copies, waits for them, and re-layouts  107 us (15%)
  other arithmetic  76.8 us (11%)
  matrix products  35.1 us (5%)
  starting transfers between devices  20.7 us (3%)
  blocking collectives  15.3 us (2%)
    all_to_all x1, waiting for transfers between devices, on_device(): pieces = lax.all_to_all(pieces, 'chan', split_axis=0, concat_axis=0)  286 us
    all_to_all x1, waiting for transfers between devices, on_device(): lax.all_to_all(spectra, 'seg', split_axis=0, concat_axis=4, tiled=True)  183 us
    cos x4, other arithmetic, transform(): table_part = jnp.concatenate([jnp.cos(angles), -jnp.sin(angles)], axis=1)  66.1 us
    reshape x1, local copies, waits for them, and re-layouts, invert(): flat = spectra.reshape(-1, spectra.shape[3] * spectra.shape[4])  27.3 us
    all_to_all x1, local copies, waits for them, and re-layouts, on_device(): lax.all_to_all(spectra, 'seg', split_axis=0, concat_axis=4, tiled=True)  26 us
    another operation x1, local copies, waits for them, and re-layouts, cross_terms(): return jnp.stack([real_part, imag_part], axis=3).astype(jnp.bfloat16)  23.5 us
    all_to_all x1, blocking collectives, on_device(): lax.all_to_all(whitened, 'seg', split_axis=3, concat_axis=1, tiled=True)  15.3 us
  transfers between devices with their start and end apart: 2, of which 2 were waited for; matrix products, arithmetic and copies ran while one was open for 1% of the time, Pallas kernels for 0%

profile of v1, /device:TPU:2, one launch (start us, length us, event | category | flops | bytes accessed | tf_op | source)
XLA Modules:
  0.0 727.0 jit_solution(270946525019661823)
XLA Ops:
  0.0 0.1 convert_reduce_fusion
  0.1 7.2 reshape.211
  7.3 82.4 %while.13 = (s32[]{:T(128)}, f32[4,256,256]{1,2,0:T(8,128)S(1)}, s32[4]{0:T(128)S(1)}, bf16[256,8192]{1,0:T(8,128)(2,1)}, s32[]{:T(128)}, /*index=5*/s32[1]{0:T(128)}, s32[1]{0:T(128)}) while((s32[]{:T(128)}, f32[4,256,256]{1,2,0:T(8,128)S(1)}, s32[4]{0:T(128)S(1)}, bf16[256,8192]{1,0:T(8,128)(2,1)}, s32[]{:T(128)}, ...), condition=%wide.region_8.9_spmd.clone, body=%wide.region_7.8_spmd.clone.sunk | while | flops 2182152192 | bytes 51119260 | solution.py:85
  7.3 0.7 dynamic_slice.19
  8.6 0.0 copy-start
  8.7 16.5 %fusion.57 = (f32[8192,128]{1,0:T(8,128)S(1)}, f32[8192,128]{1,0:T(8,128)S(1)}) fusion(s32[128]{0:T(128)S(1)} %iota_add_fusion.3), kind=kLoop, calls=%fused_computation.18.clone.1 | loop fusion | flops 15728640 | bytes 8389120 | tf_op jit(solution)/shard_map/while/body/eval_jaxpr/cos | solution.py:79
  25.2 1.3 fusion.58
  26.5 1.3 fusion.59
  27.8 0.7 dynamic_slice.19
  29.2 0.0 copy-start
  29.2 16.5 %fusion.57 = (f32[8192,128]{1,0:T(8,128)S(1)}, f32[8192,128]{1,0:T(8,128)S(1)}) fusion(s32[128]{0:T(128)S(1)} %iota_add_fusion.3), kind=kLoop, calls=%fused_computation.18.clone.1 | loop fusion | flops 15728640 | bytes 8389120 | tf_op jit(solution)/shard_map/while/body/eval_jaxpr/cos | solution.py:79
  45.7 0.0 copy-done
  45.7 1.3 fusion.58
  47.0 1.3 fusion.59
  48.4 0.7 dynamic_slice.19
  49.7 0.0 copy-start
  49.8 16.5 %fusion.57 = (f32[8192,128]{1,0:T(8,128)S(1)}, f32[8192,128]{1,0:T(8,128)S(1)}) fusion(s32[128]{0:T(128)S(1)} %iota_add_fusion.3), kind=kLoop, calls=%fused_computation.18.clone.1 | loop fusion | flops 15728640 | bytes 8389120 | tf_op jit(solution)/shard_map/while/body/eval_jaxpr/cos | solution.py:79
  66.3 1.3 fusion.58
  67.6 1.3 fusion.59
  68.9 0.7 dynamic_slice.19
  70.3 0.0 copy-start
  70.3 16.5 %fusion.57 = (f32[8192,128]{1,0:T(8,128)S(1)}, f32[8192,128]{1,0:T(8,128)S(1)}) fusion(s32[128]{0:T(128)S(1)} %iota_add_fusion.3), kind=kLoop, calls=%fused_computation.18.clone.1 | loop fusion | flops 15728640 | bytes 8389120 | tf_op jit(solution)/shard_map/while/body/eval_jaxpr/cos | solution.py:79
  86.8 1.3 fusion.58
  88.2 1.3 fusion.59
  89.7 0.4 copy.29
  90.0 0.4 reshape.213
  90.5 1.2 divide_convert_fusion.1
  91.7 0.1 stack.29
  91.8 0.1 stack.28
  91.9 0.1 pad_maximum_fusion.2
  92.0 15.3 %all_to_all.35 = bf16[128,2,2,4,128]{4,0,2,1,3:T(8,128)(2,1)S(1)} all-to-all(bf16[128,2,2,4,128]{4,0,2,1,3:T(8,128)(2,1)S(1)} %pad_maximum_fusion.2), channel_id=1, replica_groups=mesh['chan'=32,'seg'=4] {'seg'}, dimensions={3} | all-to-all | bytes 1048576 | tf_op jit(solution)/shard_map/all_to_all | solution.py:103
  107.3 0.3 copy.32
  107.6 6.2 stack.31
  113.8 8.3 %all-to-all-start.1 = ((bf16[32,128,8,2,128]{4,2,3,1,0:T(8,128)(2,1)}), bf16[32,128,8,2,128]{4,2,3,1,0:T(8,128)(2,1)}, u32[]{:S(2)}, u32[]{:S(2)}) async-start(bf16[32,128,8,2,128]{4,2,3,1,0:T(8,128)(2,1)} %stack.31), calls=%async_computation.1 | async-start | bytes 33554432 | tf_op jit(solution)/shard_map/all_to_all | solution.py:118
  122.1 0.1 copy.27
  122.2 0.1 reduce-window.9
  122.3 0.1 reduce
  122.4 0.1 copy.28
  122.5 0.1 convert_reduce_fusion.1
  122.6 0.1 select_reduce_fusion.3
  122.7 0.1 select_reduce_fusion
  122.9 0.0 copy-done.3
  122.9 0.1 select_reduce_fusion.2
  123.0 0.1 dynamic_slice.14
  123.1 0.1 dynamic_slice.13
  123.1 0.1 dynamic-slice_bitcast_fusion.1
  123.2 0.1 dynamic-slice_bitcast_fusion
  123.3 0.1 fusion.38
  123.4 0.1 compare_and_fusion.1
  123.5 285.8 %all-to-all-done.1 = bf16[32,128,8,2,128]{4,2,3,1,0:T(8,128)(2,1)} async-done(((bf16[32,128,8,2,128]{4,2,3,1,0:T(8,128)(2,1)}), bf16[32,128,8,2,128]{4,2,3,1,0:T(8,128)(2,1)}, u32[]{:S(2)}, u32[]{:S(2)}) %all-to-all-start.1) | async-done | bytes 16777248 | tf_op jit(solution)/shard_map/all_to_all | solution.py:118
  409.3 7.9 %gather_fusion = bf16[4,128,8,2,128]{4,2,3,1,0:T(8,128)(2,1)} fusion(bf16[32,128,8,2,128]{4,2,3,1,0:T(8,128)(2,1)} %all-to-all-done.1, s32[1024]{0:T(1024)S(1)} %pad_clamp_fusion), kind=kCustom, calls=%fused_computation | custom fusion | bytes 4194320 | tf_op jit(solution)/shard_map/jit(_take)/gather | solution.py:123
  417.2 4.2 copy.33
  421.4 0.3 select_select_fusion
  421.7 0.1 fusion.42
  421.9 4.9 fusion.18
  426.8 4.9 fusion.19
  431.6 6.8 pad_maximum_fusion.1
  438.4 23.5 %copy.34 = bf16[128,2,128,2,128]{2,4,1,3,0:T(8,128)(2,1)} copy(bf16[128,2,128,2,128]{0,2,4,1,3:T(8,128)(2,1)} %pad_maximum_fusion.1) | data formatting | bytes 33554432 | tf_op jit(solution)/shard_map/stack | solution.py:54
  461.9 12.4 %all-to-all-start.2 = ((bf16[128,2,128,2,128]{2,4,1,3,0:T(8,128)(2,1)}), bf16[128,2,128,2,128]{2,4,1,3,0:T(8,128)(2,1)}, u32[]{:S(2)}, u32[]{:S(2)}) async-start(bf16[128,2,128,2,128]{2,4,1,3,0:T(8,128)(2,1)} %copy.34), calls=%async_computation.2 | async-start | bytes 33554432 | tf_op jit(solution)/shard_map/all_to_all | solution.py:130
  474.4 2.5 cosine_convert_fusion
  476.9 183.0 %all-to-all-done.2 = bf16[128,2,128,2,128]{2,4,1,3,0:T(8,128)(2,1)} async-done(((bf16[128,2,128,2,128]{2,4,1,3,0:T(8,128)(2,1)}), bf16[128,2,128,2,128]{2,4,1,3,0:T(8,128)(2,1)}, u32[]{:S(2)}, u32[]{:S(2)}) %all-to-all-start.2) | async-done | bytes 16777248 | tf_op jit(solution)/shard_map/all_to_all | solution.py:130
  659.9 26.0 %copy.36 = bf16[32,2,128,2,4,128]{5,4,3,2,1,0:T(4,128)(2,1)} copy(bf16[32,2,128,2,4,128]{2,5,1,3,0,4:T(8,128)(2,1)} %bitcast.21) | data formatting | bytes 33554432 | tf_op jit(solution)/shard_map/all_to_all | solution.py:130
  686.0 27.3 %reshape.214 = bf16[8192,1024]{1,0:T(8,128)(2,1)} reshape(bf16[32,2,128,2,4,128]{5,4,3,2,1,0:T(4,128)(2,1)} %copy.36) | data formatting | bytes 33554432 | tf_op jit(solution)/shard_map/reshape | solution.py:58
  713.3 13.7 %convolution_multiply_fusion = f32[8192,256]{1,0:T(8,128)} fusion(bf16[8192,1024]{1,0:T(8,128)(2,1)} %reshape.214, bf16[512,256]{1,0:T(8,128)(2,1)S(1)} %get-tuple-element.99, bf16[512,256]{1,0:T(8,128)(2,1)S(1)} %get-tuple-element.98), kind=kOutput, calls=%fused_computation.28 | convolution fusion | flops 4298113024 | bytes 25690112 | tf_op jit(solution)/shard_map/dot_general | solution.py:59
  (25 shorter events, 0.2 us)
Async XLA Ops:
  8.6 16.5 %copy-start = (bf16[256,8192]{1,0:T(8,128)(2,1)S(1)}, bf16[256,8192]{1,0:T(8,128)(2,1)}, u32[]{:S(2)}) copy-start(bf16[256,8192]{1,0:T(8,128)(2,1)} %get-tuple-element.148) | copy-start | bytes 12582916 | tf_op jit(solution)/shard_map/while
  29.2 16.5 %copy-start = (bf16[256,8192]{1,0:T(8,128)(2,1)S(1)}, bf16[256,8192]{1,0:T(8,128)(2,1)}, u32[]{:S(2)}) copy-start(bf16[256,8192]{1,0:T(8,128)(2,1)} %get-tuple-element.148) | copy-start | bytes 12582916 | tf_op jit(solution)/shard_map/while
  49.7 16.5 %copy-start = (bf16[256,8192]{1,0:T(8,128)(2,1)S(1)}, bf16[256,8192]{1,0:T(8,128)(2,1)}, u32[]{:S(2)}) copy-start(bf16[256,8192]{1,0:T(8,128)(2,1)} %get-tuple-element.148) | copy-start | bytes 12582916 | tf_op jit(solution)/shard_map/while
  70.3 16.5 %copy-start = (bf16[256,8192]{1,0:T(8,128)(2,1)S(1)}, bf16[256,8192]{1,0:T(8,128)(2,1)}, u32[]{:S(2)}) copy-start(bf16[256,8192]{1,0:T(8,128)(2,1)} %get-tuple-element.148) | copy-start | bytes 12582916 | tf_op jit(solution)/shard_map/while
  113.8 8.3 %copy-start.2 = (s32[32]{0:T(128)S(1)}, s32[32]{0:T(128)}, u32[]{:S(2)}) copy-start(s32[32]{0:T(128)} %param.8) | copy-start | bytes 388
  113.8 8.6 %copy-start.1 = (s32[32,16]{0,1:T(8,128)S(1)}, s32[32,16]{0,1:T(8,128)}, u32[]{:S(2)}) copy-start(s32[32,16]{0,1:T(8,128)} %param.7) | copy-start | bytes 6148
  113.8 9.0 %copy-start.3 = (s32[64]{0:T(128)S(1)}, s32[64]{0:T(128)}, u32[]{:S(2)}) copy-start(s32[64]{0:T(128)} %param.9) | copy-start | bytes 772
  113.8 295.5 %all-to-all-start.1 = ((bf16[32,128,8,2,128]{4,2,3,1,0:T(8,128)(2,1)}), bf16[32,128,8,2,128]{4,2,3,1,0:T(8,128)(2,1)}, u32[]{:S(2)}, u32[]{:S(2)}) async-start(bf16[32,128,8,2,128]{4,2,3,1,0:T(8,128)(2,1)} %stack.31), calls=%async_computation.1 | async-start | bytes 33554432 | tf_op jit(solution)/shard_map/all_to_all | solution.py:118
  461.9 198.0 %all-to-all-start.2 = ((bf16[128,2,128,2,128]{2,4,1,3,0:T(8,128)(2,1)}), bf16[128,2,128,2,128]{2,4,1,3,0:T(8,128)(2,1)}, u32[]{:S(2)}, u32[]{:S(2)}) async-start(bf16[128,2,128,2,128]{2,4,1,3,0:T(8,128)(2,1)} %copy.34), calls=%async_computation.2 | async-start | bytes 33554432 | tf_op jit(solution)/shard_map/all_to_all | solution.py:130
